TPU v7x, 512 devices: a whole 4x8x8 slice. The times are simulated.
512 devices in a mesh: section: 8 (over y), dp: 64 (over z, x, core).
Axes of the slice: x: 4, y: 8, z: 8, core: 2. Of those that a mesh axis runs over, the one named last changes fastest.
Arguments:
- fresh_acts: bfloat16 [3, 128, 8192], P(None, None, 'dp'), may hold values from -36 to 36
- carried: bfloat16 [8, 128, 8192], P('section', None, 'dp'), may hold values from -36 to 36
- norm_gain: float32 [8, 8192], P('section'), may hold values from 0.1 to 1.9
- w_in: bfloat16 [8, 3, 4096, 8192], P('section', None, 'dp'), may hold values from -0.0625 to 0.0625
- short_filter: float32 [8, 3, 4096, 3], P('section', None, 'dp'), may hold values from -3 to 3
- filter_taps: float32 [8, 4096, 128], P('section', 'dp'), may hold values from -0.9 to 0.9
- decay_rate: float32 [8, 4096], P('section', 'dp'), may hold values from 0.01 to 0.12
- w_out: bfloat16 [8, 4096, 8192], P('section', None, 'dp'), may hold values from -0.09375 to 0.09375
Outputs:
- section_outputs: bfloat16 [8, 3, 128, 8192], P('section', None, None, 'dp')
All inputs are finite; a program needn't handle non-finite values.
Results may differ from a plain program's by a relative error of at most 0.011.
Values may be sent and summed in bfloat16 or wider, within the bound.
A program may use at most 64 MiB of HBM per device.

v0:
```python
import jax
import jax.numpy as jnp
from jax import lax
from jax.sharding import PartitionSpec as P

EPS = 1e-06


def shifted(value, axis, steps):
    count = lax.axis_size(axis)
    pairs = [(source, (source + steps) % count) for source in range(count)]
    return lax.ppermute(value, axis, pairs)


def build_toeplitz(tap_values, decay_rate, tok_len):
    tap_count = tap_values.shape[1]
    lag_grid = jnp.arange(tok_len)[:, None] - jnp.arange(tok_len)[None, :]
    onehot = (lag_grid[:, :, None] == jnp.arange(tap_count)[None, None, :]).astype(jnp.float32)
    filter_vals = tap_values * jnp.exp(
        -decay_rate[:, None] * jnp.arange(tap_count, dtype=jnp.float32)[None, :]
    )
    return jnp.einsum("cj,tsj->cts", filter_vals, onehot, precision=lax.Precision.HIGHEST)


def mixing(u_proj, short_taps, toeplitz):
    tok_len = u_proj.shape[0]
    tap_count = short_taps.shape[2]
    padded = jnp.pad(u_proj, ((tap_count - 1, 0), (0, 0), (0, 0)))
    mixed_out = short_taps[:, :, 0] * u_proj
    for j in range(1, tap_count):
        mixed_out = (
            mixed_out
            + short_taps[:, :, j] * padded[tap_count - 1 - j : tap_count - 1 - j + tok_len]
        )
    query_part = mixed_out[:, 0]
    product = mixed_out[:, 1] * mixed_out[:, 2]
    long_conv = jnp.einsum("cts,sc->tc", toeplitz, product, precision=lax.Precision.HIGHEST)
    return (query_part * long_conv).astype(jnp.bfloat16)


def contract_rows(normed, weight_rows):
    return lax.dot_general(
        normed, weight_rows, (((1,), (1,)), ((), ())), preferred_element_type=jnp.float32
    )


def body(fresh_acts, carried, norm_gain, w_in, short_filter, filter_taps, decay_rate, w_out):
    section_idx = lax.axis_index("section")
    section_count = lax.axis_size("section")
    is_first = section_idx == 0
    tick_count = fresh_acts.shape[0]
    tok_len = fresh_acts.shape[1]
    feat_dev = fresh_acts.shape[2]
    model_width = norm_gain.shape[1]
    chan_dev = w_in.shape[2]
    gain_row = norm_gain[0]
    w_in_flat = w_in[0].reshape(3 * chan_dev, model_width)
    w_out_local = w_out[0]
    short_taps = short_filter[0]
    toeplitz = build_toeplitz(filter_taps[0], decay_rate[0], tok_len)
    own_start = lax.axis_index("dp") * feat_dev
    start_slice = jnp.where(is_first, fresh_acts[0], carried[0])
    results = []
    is_last = section_idx == section_count - 1
    full_rows = lax.all_gather(start_slice, "dp", axis=1, tiled=True)
    for k in range(tick_count):
        widened = full_rows.astype(jnp.float32)
        normed = (widened * gain_row).astype(jnp.bfloat16)
        from_proj_acc = contract_rows(normed, w_in_flat)
        from_sum_sq = jnp.sum(widened * widened, axis=1)
        from_own_slice = lax.dynamic_slice_in_dim(full_rows, own_start, feat_dev, 1)
        factor = lax.rsqrt(from_sum_sq / model_width + EPS)
        u_proj = (from_proj_acc * factor[:, None]).reshape(tok_len, 3, chan_dev)
        y_local = mixing(u_proj, short_taps, toeplitz)
        out_acc = jnp.dot(
            lax.all_gather(y_local, "dp", axis=1, tiled=True),
            w_out_local,
            preferred_element_type=jnp.float32,
        )
        produced = (from_own_slice.astype(jnp.float32) + out_acc).astype(jnp.bfloat16)
        results.append(produced)
        if k + 1 < tick_count:
            source = jnp.where(is_last, fresh_acts[k + 1], produced)
            gathered = lax.all_gather(source, "dp", axis=1, tiled=True)
            full_rows = shifted(gathered, "section", 1)
    return jnp.stack(results)[None]


def solution(mesh):
    return jax.shard_map(
        body,
        mesh=mesh,
        in_specs=(
            P(None, None, "dp"),
            P("section", None, "dp"),
            P("section", None),
            P("section", None, "dp", None),
            P("section", None, "dp", None),
            P("section", "dp", None),
            P("section", "dp"),
            P("section", None, "dp"),
        ),
        out_specs=P("section", None, None, "dp"),
        check_vma=False,
    )
```

profile of v0, /device:TPU:1, one launch (start us, length us, event | category | flops | bytes accessed | tf_op | source)
XLA Modules:
  0.0 632.6 jit_solution(17019697142126312985)
XLA Ops:
  6.5 0.0 copy-start
  6.5 0.0 all-gather.18.cloned.1.call-start
  6.5 1.5 slice_select_fusion
  8.1 0.0 all-gather.18.cloned.1.call-update
  8.1 0.0 all-gather.8.cloned.1.call-start
  8.1 0.7 copy.24
  8.9 0.7 negate_bitcast_fusion
  9.5 8.1 %fusion = f32[64,128,128]{2,0,1:T(8,128)} fusion(s32[128,128]{1,0:T(8,128)S(1)} %iota_subtract_fusion, f32[1,64,128]{2,1,0:T(8,128)} %param.13, f32[64]{0:T(128)S(1)} %negate_bitcast_fusion), kind=kOutput, calls=%fused_computation.1 | convolution fusion | flops 1612726272 | bytes 4292864 | tf_op jit(solution)/shard_map/cj,tsj->cts/dot_general | solution.py:22
  17.6 0.0 copy-start.7
  17.6 5.4 copy.10
  23.0 72.1 %all-gather.18.cloned.1.call-done = bf16[1,128,8192]{2,1,0:T(8,128)(2,1)} async-done(((bf16[1,128,128]{2,1,0:T(8,128)(2,1)}), bf16[1,128,8192]{2,1,0:T(8,128)(2,1)}) %all-gather.18.cloned.1.call-update) | async-done | bytes 2097168 | tf_op jit(solution)/shard_map/all_gather | solution.py:65
  95.1 2.1 fusion.6
  97.2 0.0 copy-start.1
  97.2 0.0 copy-done
  97.2 0.0 copy-done.7
  97.2 2.7 fusion.24
  100.0 0.0 copy-start.6
  100.0 0.2 fusion.35
  100.2 0.0 copy-done.1
  100.2 3.7 fusion.60
  103.9 0.6 fusion.51
  104.5 0.0 all-gather.8.cloned.1.call-update
  104.5 0.0 all-gather.10.cloned.1.call-start
  104.6 81.2 %all-gather.8.cloned.1.call-done = bf16[128,4096]{0,1:T(8,128)(2,1)} async-done(((bf16[128,64]{0,1:T(8,128)(2,1)}), bf16[128,4096]{0,1:T(8,128)(2,1)}) %all-gather.8.cloned.1.call-update) | async-done | bytes 1048592 | tf_op jit(solution)/shard_map/all_gather | solution.py:76
  185.8 0.0 copy-done.6
  185.8 2.6 bitcast_select_fusion.1
  188.5 0.0 all-gather.10.cloned.1.call-update
  188.5 0.0 all-gather.12.cloned.1.call-start
  188.5 76.4 %all-gather.10.cloned.1.call-done = bf16[128,8192]{1,0:T(8,128)(2,1)} async-done(((bf16[128,128]{1,0:T(8,128)(2,1)}), bf16[128,8192]{1,0:T(8,128)(2,1)}) %all-gather.10.cloned.1.call-update) | async-done | bytes 2097168 | tf_op jit(solution)/shard_map/all_gather | solution.py:84
  264.9 3.3 collective-permute-start
  268.2 47.0 %collective-permute-done = bf16[128,8192]{1,0:T(8,128)(2,1)S(1)} collective-permute-done((bf16[128,8192]{1,0:T(8,128)(2,1)}, bf16[128,8192]{1,0:T(8,128)(2,1)S(1)}, u32[]{:S(2)}, u32[]{:S(2)}) %collective-permute-start) | collective-permute-done | bytes 2097184 | tf_op jit(solution)/shard_map/ppermute | solution.py:12
  315.2 0.0 copy-start.4
  315.2 0.5 fusion.2
  315.7 0.0 copy-start.2
  315.7 1.1 fusion.18
  316.8 0.0 copy-done.4
  316.8 0.2 fusion.39
  317.0 1.1 copy-done.2
  318.1 3.6 fusion.61
  321.8 0.6 fusion.49
  322.4 0.0 all-gather.12.cloned.1.call-update
  322.4 0.0 all-gather.14.cloned.1.call-start
  322.5 82.1 %all-gather.12.cloned.1.call-done = bf16[128,4096]{0,1:T(8,128)(2,1)} async-done(((bf16[128,64]{0,1:T(8,128)(2,1)}), bf16[128,4096]{0,1:T(8,128)(2,1)}) %all-gather.12.cloned.1.call-update) | async-done | bytes 1048592 | tf_op jit(solution)/shard_map/all_gather | solution.py:76
  404.5 2.6 bitcast_select_fusion
  407.2 0.0 all-gather.14.cloned.1.call-update
  407.2 0.0 all-gather.16.cloned.1.call-start
  407.3 76.3 %all-gather.14.cloned.1.call-done = bf16[128,8192]{1,0:T(8,128)(2,1)} async-done(((bf16[128,128]{1,0:T(8,128)(2,1)}), bf16[128,8192]{1,0:T(8,128)(2,1)}) %all-gather.14.cloned.1.call-update) | async-done | bytes 2097168 | tf_op jit(solution)/shard_map/all_gather | solution.py:84
  483.5 3.1 collective-permute-start.1
  486.6 47.2 %collective-permute-done.1 = bf16[128,8192]{1,0:T(8,128)(2,1)S(1)} collective-permute-done((bf16[128,8192]{1,0:T(8,128)(2,1)}, bf16[128,8192]{1,0:T(8,128)(2,1)S(1)}, u32[]{:S(2)}, u32[]{:S(2)}) %collective-permute-start.1) | collective-permute-done | bytes 2097184 | tf_op jit(solution)/shard_map/ppermute | solution.py:12
  533.8 0.0 copy-start.5
  533.8 0.5 fusion.4
  534.3 0.0 copy-start.3
  534.3 1.1 fusion.21
  535.4 0.0 copy-done.5
  535.4 0.2 fusion.43
  535.6 1.1 copy-done.3
  536.7 3.6 fusion.62
  540.4 0.6 fusion.47
  541.0 0.0 all-gather.16.cloned.1.call-update
  541.0 82.1 %all-gather.16.cloned.1.call-done = bf16[128,4096]{0,1:T(8,128)(2,1)} async-done(((bf16[128,64]{0,1:T(8,128)(2,1)}), bf16[128,4096]{0,1:T(8,128)(2,1)}) %all-gather.16.cloned.1.call-update) | async-done | bytes 1048592 | tf_op jit(solution)/shard_map/all_gather | solution.py:76
  623.1 2.0 fusion.45
  625.1 0.7 maximum_bitcast_fusion
  (10 shorter events, 0.1 us)
Async XLA Ops:
  6.5 90.7 %copy-start = (bf16[1,3,64,8192]{3,2,1,0:T(8,128)(2,1)S(1)}, bf16[1,3,64,8192]{3,2,1,0:T(8,128)(2,1)}, u32[]{:S(2)}) copy-start(bf16[1,3,64,8192]{3,2,1,0:T(8,128)(2,1)} %param.11) | copy-start | bytes 9437188
  6.5 88.6 %all-gather.18.cloned.1.call-start = ((), (), s32[]{:S(2)}) async-start(), calls=%async_computation.5 | async-start | bytes 2129920 | tf_op jit(solution)/shard_map/all_gather | solution.py:65
  8.1 177.7 %all-gather.8.cloned.1.call-start = ((), (), s32[]{:S(2)}) async-start(), calls=%async_computation | async-start | bytes 1064960 | tf_op jit(solution)/shard_map/all_gather | solution.py:76
  17.6 79.6 %copy-start.7 = (f32[1,8192]{1,0:T(1,128)S(1)}, f32[1,8192]{1,0:T(1,128)}, u32[]{:S(2)}) copy-start(f32[1,8192]{1,0:T(1,128)} %param.10) | copy-start | bytes 98308
  97.2 3.0 copy-start.1
  100.0 85.8 %copy-start.6 = (bf16[3,128,128]{2,1,0:T(8,128)(2,1)S(1)}, bf16[3,128,128]{2,1,0:T(8,128)(2,1)}, u32[]{:S(2)}) copy-start(bf16[3,128,128]{2,1,0:T(8,128)(2,1)} %param.8) | copy-start | bytes 294916
  104.5 160.4 %all-gather.10.cloned.1.call-start = ((), (), s32[]{:S(2)}) async-start(), calls=%async_computation.1 | async-start | bytes 2129920 | tf_op jit(solution)/shard_map/all_gather | solution.py:84
  188.5 216.1 %all-gather.12.cloned.1.call-start = ((), (), s32[]{:S(2)}) async-start(), calls=%async_computation.2 | async-start | bytes 1064960 | tf_op jit(solution)/shard_map/all_gather | solution.py:76
  264.9 50.3 %collective-permute-start = (bf16[128,8192]{1,0:T(8,128)(2,1)}, bf16[128,8192]{1,0:T(8,128)(2,1)S(1)}, u32[]{:S(2)}, u32[]{:S(2)}) collective-permute-start(bf16[128,8192]{1,0:T(8,128)(2,1)} %all-gather.10.cloned.1.call-done), channel_id=1, source_target_pairs={{0,64},{64,128},{128,192},{192,256},{256,320},{320,384},{384,448},... | collective-permute-start | bytes 6291464 | tf_op jit(solution)/shard_map/ppermute | solution.py:12
  315.2 1.6 copy-start.4
  315.7 2.4 copy-start.2
  322.4 161.1 %all-gather.14.cloned.1.call-start = ((), (), s32[]{:S(2)}) async-start(), calls=%async_computation.3 | async-start | bytes 2129920 | tf_op jit(solution)/shard_map/all_gather | solution.py:84
  407.2 215.9 %all-gather.16.cloned.1.call-start = ((), (), s32[]{:S(2)}) async-start(), calls=%async_computation.4 | async-start | bytes 1064960 | tf_op jit(solution)/shard_map/all_gather | solution.py:76
  483.5 50.3 %collective-permute-start.1 = (bf16[128,8192]{1,0:T(8,128)(2,1)}, bf16[128,8192]{1,0:T(8,128)(2,1)S(1)}, u32[]{:S(2)}, u32[]{:S(2)}) collective-permute-start(bf16[128,8192]{1,0:T(8,128)(2,1)} %all-gather.14.cloned.1.call-done), channel_id=1, source_target_pairs={{0,64},{64,128},{128,192},{192,256},{256,320},{320,384},{384,448},... | collective-permute-start | bytes 6291464 | tf_op jit(solution)/shard_map/ppermute | solution.py:12
  533.8 1.6 copy-start.5
  534.3 2.4 copy-start.3
Sparse Core Ops, SparseCore 0:
  10.6 84.5 all-gather.17
  104.6 81.1 all-gather.7
  189.0 75.8 all-gather.9
  322.6 81.9 all-gather.11
  407.6 75.8 all-gather.13
  541.1 81.9 all-gather.15
where the time goes:
time: 633 us
  waiting for transfers between devices  564 us (89%)
  matrix products  31.2 us (5%)
  between operations  13.7 us (2%)
  other arithmetic  8.37 us (1%)
  local copies, waits for them, and re-layouts  8.34 us (1%)
  starting transfers between devices  6.59 us (1%)
    all_gather x3, waiting for transfers between devices, body(): lax.all_gather(y_local, 'dp', axis=1, tiled=True)  245 us
    all_gather x2, waiting for transfers between devices, body(): gathered = lax.all_gather(source, 'dp', axis=1, tiled=True)  153 us
    ppermute x2, waiting for transfers between devices, shifted(): return lax.ppermute(value, axis, pairs)  94.2 us
    all_gather x1, waiting for transfers between devices, body(): full_rows = lax.all_gather(start_slice, 'dp', axis=1, tiled=True)  72.1 us
  transfers between devices with their start and end apart: 8, of which 8 were waited for; matrix products, arithmetic and copies ran while one was open for 2% of the time, Pallas kernels for 0%

commit v1 on v0

--- a/solution.py
+++ b/solution.py
@@ -81,7 +81,8 @@
         results.append(produced)
         if k + 1 < tick_count:
             source = jnp.where(is_last, fresh_acts[k + 1], produced)
-            gathered = lax.all_gather(source, "dp", axis=1, tiled=True)
+            repeated = jnp.stack([source] * lax.axis_size("dp"))
+            gathered = jnp.concatenate(lax.all_to_all(repeated, "dp", 0, 0), axis=1)
             full_rows = shifted(gathered, "section", 1)
     return jnp.stack(results)[None]
 

time: 633 us -> 589 us (0.930)
  waiting for transfers between devices: 564 us -> 408 us
  blocking collectives: 0 us -> 112 us
    all_gather x2 -> x0, waiting for transfers between devices: 153 us -> none  [body(): gathered = lax.all_gather(source, 'dp', axis=1, tiled=True)]
    all_to_all x0 -> x2, blocking collectives: none -> 112 us  [body(): gathered = jnp.concatenate(lax.all_to_all(repeated, 'dp', 0, 0), axis=1)]
  transfers between devices with their start and end apart: 8 -> 6, of which waited for: 8 -> 6; matrix products, arithmetic and copies ran while one was open for 2% -> 3% of each run, Pallas kernels for 0% -> 0%
where the time goes in v1:
time: 589 us
  waiting for transfers between devices  408 us (69%)
  blocking collectives  112 us (19%)
  matrix products  30 us (5%)
  between operations  13.4 us (2%)
  local copies, waits for them, and re-layouts  9.97 us (2%)
  other arithmetic  8.37 us (1%)
  starting transfers between devices  6.76 us (1%)
    all_gather x3, waiting for transfers between devices, body(): lax.all_gather(y_local, 'dp', axis=1, tiled=True)  247 us
    all_to_all x2, blocking collectives, body(): gathered = jnp.concatenate(lax.all_to_all(repeated, 'dp', 0, 0), axis=1)  112 us
    ppermute x2, waiting for transfers between devices, shifted(): return lax.ppermute(value, axis, pairs)  89.5 us
    all_gather x1, waiting for transfers between devices, body(): full_rows = lax.all_gather(start_slice, 'dp', axis=1, tiled=True)  72.1 us
  transfers between devices with their start and end apart: 6, of which 6 were waited for; matrix products, arithmetic and copies ran while one was open for 3% of the time, Pallas kernels for 0%

profile of v1, /device:TPU:1, one launch (start us, length us, event | category | flops | bytes accessed | tf_op | source)
XLA Modules:
  0.0 588.8 jit_solution(3853755436859652920)
XLA Ops:
  6.5 0.0 copy-start
  6.5 0.0 all-gather.12.cloned.1.call-start
  6.5 1.5 slice_select_fusion
  8.1 0.0 all-gather.12.cloned.1.call-update
  8.1 0.0 all-gather.6.cloned.1.call-start
  8.1 0.7 copy.30
  8.9 0.7 negate_bitcast_fusion
  9.5 8.1 %fusion = f32[64,128,128]{2,0,1:T(8,128)} fusion(s32[128,128]{1,0:T(8,128)S(1)} %iota_subtract_fusion, f32[1,64,128]{2,1,0:T(8,128)} %param.13, f32[64]{0:T(128)S(1)} %negate_bitcast_fusion), kind=kOutput, calls=%fused_computation.1 | convolution fusion | flops 1612726272 | bytes 4292864 | tf_op jit(solution)/shard_map/cj,tsj->cts/dot_general | solution.py:22
  17.6 0.0 copy-start.7
  17.6 5.5 copy.12
  23.1 72.1 %all-gather.12.cloned.1.call-done = bf16[1,128,8192]{2,1,0:T(8,128)(2,1)} async-done(((bf16[1,128,128]{2,1,0:T(8,128)(2,1)}), bf16[1,128,8192]{2,1,0:T(8,128)(2,1)}) %all-gather.12.cloned.1.call-update) | async-done | bytes 2097168 | tf_op jit(solution)/shard_map/all_gather | solution.py:65
  95.1 2.1 fusion.6
  97.2 0.0 copy-start.1
  97.2 0.0 copy-done
  97.2 0.0 copy-done.7
  97.2 2.7 fusion.24
  100.0 0.0 copy-start.6
  100.0 0.2 fusion.35
  100.2 0.0 copy-done.1
  100.2 3.7 fusion.60
  103.9 0.6 fusion.51
  104.5 0.0 all-gather.6.cloned.1.call-update
  104.5 0.0 all-gather.8.cloned.1.call-start
  104.6 81.2 %all-gather.6.cloned.1.call-done = bf16[128,4096]{0,1:T(8,128)(2,1)} async-done(((bf16[128,64]{0,1:T(8,128)(2,1)}), bf16[128,4096]{0,1:T(8,128)(2,1)}) %all-gather.6.cloned.1.call-update) | async-done | bytes 1048592 | tf_op jit(solution)/shard_map/all_gather | solution.py:76
  185.8 0.0 copy-done.6
  185.8 2.0 bitcast_select_fusion.1
  187.8 0.5 stack.13
  188.3 56.0 %all_to_all.10 = bf16[64,128,128]{2,1,0:T(8,128)(2,1)S(1)} all-to-all(bf16[64,128,128]{2,1,0:T(8,128)(2,1)S(1)} %stack.13), channel_id=1, replica_groups=mesh['section'=8,'dp'=64] {'dp'}, dimensions={0} | all-to-all | bytes 4194304 | tf_op jit(solution)/shard_map/all_to_all | solution.py:85
  244.4 0.3 copy_bitcast_fusion.1
  244.7 3.3 collective-permute-start
  248.0 44.8 %collective-permute-done = bf16[128,8192]{1,0:T(8,128)(2,1)S(1)} collective-permute-done((bf16[128,8192]{1,0:T(8,128)(2,1)S(1)}, bf16[128,8192]{1,0:T(8,128)(2,1)S(1)}, u32[]{:S(2)}, u32[]{:S(2)}) %collective-permute-start) | collective-permute-done | bytes 2097184 | tf_op jit(solution)/shard_map/ppermute | solution.py:12
  292.8 0.0 copy-start.4
  292.8 0.5 fusion.2
  293.2 0.0 copy-start.2
  293.3 1.1 fusion.18
  294.4 0.0 copy-done.4
  294.4 0.2 fusion.39
  294.6 1.1 copy-done.2
  295.7 3.6 fusion.61
  299.3 0.6 fusion.49
  300.0 0.0 all-gather.8.cloned.1.call-update
  300.0 0.0 all-gather.10.cloned.1.call-start
  300.0 82.7 %all-gather.8.cloned.1.call-done = bf16[128,4096]{0,1:T(8,128)(2,1)} async-done(((bf16[128,64]{0,1:T(8,128)(2,1)}), bf16[128,4096]{0,1:T(8,128)(2,1)}) %all-gather.8.cloned.1.call-update) | async-done | bytes 1048592 | tf_op jit(solution)/shard_map/all_gather | solution.py:76
  382.7 2.0 bitcast_select_fusion
  384.7 0.5 stack.15
  385.2 56.0 %all_to_all.11 = bf16[64,128,128]{2,1,0:T(8,128)(2,1)S(1)} all-to-all(bf16[64,128,128]{2,1,0:T(8,128)(2,1)S(1)} %stack.15), channel_id=1, replica_groups=mesh['section'=8,'dp'=64] {'dp'}, dimensions={0} | all-to-all | bytes 4194304 | tf_op jit(solution)/shard_map/all_to_all | solution.py:85
  441.2 0.3 copy_bitcast_fusion
  441.6 3.3 collective-permute-start.1
  444.9 44.7 %collective-permute-done.1 = bf16[128,8192]{1,0:T(8,128)(2,1)S(1)} collective-permute-done((bf16[128,8192]{1,0:T(8,128)(2,1)S(1)}, bf16[128,8192]{1,0:T(8,128)(2,1)S(1)}, u32[]{:S(2)}, u32[]{:S(2)}) %collective-permute-start.1) | collective-permute-done | bytes 2097184 | tf_op jit(solution)/shard_map/ppermute | solution.py:12
  489.6 0.0 copy-start.5
  489.6 0.5 fusion.4
  490.1 0.0 copy-start.3
  490.1 1.1 fusion.21
  491.2 0.0 copy-done.5
  491.2 0.2 fusion.43
  491.5 1.1 copy-done.3
  492.6 3.6 fusion.62
  496.2 0.6 fusion.47
  496.8 0.0 all-gather.10.cloned.1.call-update
  496.9 82.7 %all-gather.10.cloned.1.call-done = bf16[128,4096]{0,1:T(8,128)(2,1)} async-done(((bf16[128,64]{0,1:T(8,128)(2,1)}), bf16[128,4096]{0,1:T(8,128)(2,1)}) %all-gather.10.cloned.1.call-update) | async-done | bytes 1048592 | tf_op jit(solution)/shard_map/all_gather | solution.py:76
  579.6 2.0 fusion.45
  581.6 0.7 maximum_bitcast_fusion
  (10 shorter events, 0.1 us)
Async XLA Ops:
  6.5 90.7 %copy-start = (bf16[1,3,64,8192]{3,2,1,0:T(8,128)(2,1)S(1)}, bf16[1,3,64,8192]{3,2,1,0:T(8,128)(2,1)}, u32[]{:S(2)}) copy-start(bf16[1,3,64,8192]{3,2,1,0:T(8,128)(2,1)} %param.11) | copy-start | bytes 9437188
  6.5 88.6 %all-gather.12.cloned.1.call-start = ((), (), s32[]{:S(2)}) async-start(), calls=%async_computation.5 | async-start | bytes 2129920 | tf_op jit(solution)/shard_map/all_gather | solution.py:65
  8.1 177.7 %all-gather.6.cloned.1.call-start = ((), (), s32[]{:S(2)}) async-start(), calls=%async_computation.2 | async-start | bytes 1064960 | tf_op jit(solution)/shard_map/all_gather | solution.py:76
  17.6 79.6 %copy-start.7 = (f32[1,8192]{1,0:T(1,128)S(1)}, f32[1,8192]{1,0:T(1,128)}, u32[]{:S(2)}) copy-start(f32[1,8192]{1,0:T(1,128)} %param.10) | copy-start | bytes 98308
  97.2 3.0 copy-start.1
  100.0 85.8 %copy-start.6 = (bf16[3,128,128]{2,1,0:T(8,128)(2,1)S(1)}, bf16[3,128,128]{2,1,0:T(8,128)(2,1)}, u32[]{:S(2)}) copy-start(bf16[3,128,128]{2,1,0:T(8,128)(2,1)} %param.8) | copy-start | bytes 294916
  104.5 278.2 %all-gather.8.cloned.1.call-start = ((), (), s32[]{:S(2)}) async-start(), calls=%async_computation.3 | async-start | bytes 1064960 | tf_op jit(solution)/shard_map/all_gather | solution.py:76
  244.7 48.1 %collective-permute-start = (bf16[128,8192]{1,0:T(8,128)(2,1)S(1)}, bf16[128,8192]{1,0:T(8,128)(2,1)S(1)}, u32[]{:S(2)}, u32[]{:S(2)}) collective-permute-start(bf16[128,8192]{1,0:T(8,128)(2,1)S(1)} %copy_bitcast_fusion.1), channel_id=1, source_target_pairs={{0,64},{64,128},{128,192},{192,256},{256,320},{320,384},{384,448},... | collective-permute-start | bytes 6291464 | tf_op jit(solution)/shard_map/ppermute | solution.py:12
  292.8 1.6 copy-start.4
  293.2 2.4 copy-start.2
  300.0 279.6 %all-gather.10.cloned.1.call-start = ((), (), s32[]{:S(2)}) async-start(), calls=%async_computation.4 | async-start | bytes 1064960 | tf_op jit(solution)/shard_map/all_gather | solution.py:76
  441.6 48.1 %collective-permute-start.1 = (bf16[128,8192]{1,0:T(8,128)(2,1)S(1)}, bf16[128,8192]{1,0:T(8,128)(2,1)S(1)}, u32[]{:S(2)}, u32[]{:S(2)}) collective-permute-start(bf16[128,8192]{1,0:T(8,128)(2,1)S(1)} %copy_bitcast_fusion), channel_id=1, source_target_pairs={{0,64},{64,128},{128,192},{192,256},{256,320},{320,384},{384,448},... | collective-permute-start | bytes 6291464 | tf_op jit(solution)/shard_map/ppermute | solution.py:12
  489.6 1.6 copy-start.5
  490.1 2.4 copy-start.3
Sparse Core Ops, SparseCore 0:
  10.6 84.5 all-gather.11
  104.6 81.1 all-gather.5
  300.1 82.5 all-gather.7
  497.0 82.5 all-gather.9
